TPU v7x, 768 devices: a whole 4x8x12 slice. The times are simulated.
768 devices in a mesh: item: 32 (over x, y_lo, core), split: 24 (over y_hi, z).
Axes of the slice: x: 4, y: 8 (y_hi: 2, y_lo: 4; y = y_hi * 4 + y_lo), z: 12, core: 2. Of those that a mesh axis runs over, the one named last changes fastest.
Arguments:
- item_emb: float32 [16384, 128], P('item'), may hold values from -0.046875 to 0.046875
- confidences: bfloat16 [32, 24, 4, 16, 8, 128], P('item', 'split'), may hold values from 1 to 64
- user_block: int32 [32, 24, 4, 16], P('item', 'split'), may hold values from 0 to 2
- item_block: int32 [32, 24, 4, 16], P('item', 'split'), may hold values from 0 to 3
- block_age: int32 [32, 24, 4, 16], P('item', 'split'), may hold values from 0 to 15
- block_count: int32 [32, 24, 4], P('item', 'split'), may hold values from 8 to 16, as said below
Outputs:
- user_emb: float32 [768, 128], P('item')
Inputs may be any that keep to these rules, and one draw needn't show every extreme that they name: `block_count`: every device has 16 live slots at some window offset in some draw; some device has them in every draw.
All inputs are finite; a program needn't handle non-finite values.
Results may differ from a plain program's by a relative error of at most 0.0003.
Values sent between devices are 32-bit elements; how exact they have to be, the bound alone decides.
A program may use at most 32 MiB of HBM per device.

v0:
```python
import jax
import jax.numpy as jnp
from jax import lax
from jax.sharding import PartitionSpec as P

USER_BLOCKS = 3
STEPS = 4
CG_ITERS = 3


ridge_weight = 0.1


def shifted(value, axis, steps):
    count = lax.axis_size(axis)
    pairs = [(source, (source + steps) % count) for source in range(count)]
    return lax.ppermute(value, axis, pairs)


def conjugate(matrix, right):
    solution = jnp.zeros_like(right)
    residual = right
    direction = right
    norm_now = jnp.sum(residual * residual, axis=1)
    for iteration in range(CG_ITERS):
        image = jnp.einsum("ude,ue->ud", matrix, direction, precision=lax.Precision.HIGHEST)
        step_size = norm_now / jnp.sum(direction * image, axis=1)
        solution = solution + step_size[:, None] * direction
        residual = residual - step_size[:, None] * image
        norm_next = jnp.sum(residual * residual, axis=1)
        direction = residual + (norm_next / norm_now)[:, None] * direction
        norm_now = norm_next
    return solution


def body(item_emb, confidences, user_block, item_block, block_age, block_count):
    features = item_emb.shape[1]
    block_users = confidences.shape[4]
    block_items = confidences.shape[5]
    users_dev = USER_BLOCKS * block_users

    def block_parts(current_rows, loop_step, position):
        user_start = user_block[0, 0, loop_step, position] * block_users
        item_start = item_block[0, 0, loop_step, position] * block_items
        recency = 2.0 / (2.0 + block_age[0, 0, loop_step, position].astype(jnp.float32))
        item_rows = lax.dynamic_slice_in_dim(current_rows, item_start, block_items, 0)
        weights = (
            lax.dynamic_index_in_dim(
                confidences[0, 0, loop_step], position, 0, keepdims=False
            ).astype(jnp.float32)
            * recency
        )
        return (user_start, recency, item_rows, weights)

    local_gram = jnp.dot(
        item_emb.T, item_emb, precision=lax.Precision.HIGHEST, preferred_element_type=jnp.float32
    )
    total_gram = lax.psum(local_gram, "item")
    base = total_gram + ridge_weight * jnp.eye(features, dtype=jnp.float32)
    window_shards = [item_emb]
    current_rows = item_emb
    for loop_step in range(1, STEPS):
        current_rows = shifted(current_rows, "item", 1)
        window_shards.append(current_rows)
    carried = (
        jnp.zeros((users_dev, features, features), jnp.float32),
        jnp.zeros((users_dev, features), jnp.float32),
    )
    for loop_step in range(STEPS):
        add_current_rows = window_shards[loop_step]

        def add_block(position, carried_now):
            user_gram, user_right = carried_now
            user_start, recency, item_rows, weights = block_parts(
                add_current_rows, loop_step, position
            )
            weighted = weights[:, None, :] * item_rows.T[None]
            correction = jnp.dot(
                weighted.reshape(block_users * features, block_items),
                item_rows,
                precision=lax.Precision.HIGHEST,
                preferred_element_type=jnp.float32,
            ).reshape(block_users, features, features)
            right_term = jnp.dot(
                weights + recency,
                item_rows,
                precision=lax.Precision.HIGHEST,
                preferred_element_type=jnp.float32,
            )
            old_gram = lax.dynamic_slice_in_dim(user_gram, user_start, block_users, 0)
            user_gram = lax.dynamic_update_slice_in_dim(
                user_gram, old_gram + correction, user_start, 0
            )
            old_right = lax.dynamic_slice_in_dim(user_right, user_start, block_users, 0)
            user_right = lax.dynamic_update_slice_in_dim(
                user_right, old_right + right_term, user_start, 0
            )
            return (user_gram, user_right)

        carried = lax.fori_loop(0, block_count[0, 0, loop_step], add_block, carried)
    user_gram, user_right = carried
    summed_gram, summed_right = lax.psum((user_gram, user_right), "split")
    solution = conjugate(summed_gram + base[None], summed_right)
    return solution


def solution(mesh):
    placed = (
        P("item", None),
        P("item", "split", None, None, None, None),
        P("item", "split", None, None),
        P("item", "split", None, None),
        P("item", "split", None, None),
        P("item", "split", None),
    )
    return jax.shard_map(
        body, mesh=mesh, in_specs=placed, out_specs=P("item", None), check_vma=False
    )
```

profile of v0, /device:TPU:6, one launch (start us, length us, event | category | flops | bytes accessed | tf_op | source)
XLA Modules:
  0.0 861.7 jit_solution(1099663050882223773)
XLA Ops:
  6.6 2.1 collective-permute-start
  8.7 2.3 fusion.70
  11.0 1.5 fusion.69
  12.7 80.4 %while.48 = (s32[]{:T(128)}, f32[24,128,128]{2,1,0:T(8,128)S(1)}, f32[24,128]{1,0:T(8,128)S(1)}, s32[]{:T(128)}, s32[1,1,4,16]{3,2,1,0:T(4,128)S(1)}, /*index=5*...) while((s32[]{:T(128)}, f32[24,128,128]{2,1,0:T(8,128)S(1)}, ...), condition=%wide.region_1.2_spmd, body=%wide.region_0.0_spmd.sunk | while | flops 203167760 | bytes 1594699 | solution.py:100
  93.2 1.9 collective-permute-start.1
  95.1 128.4 %while.49 = (s32[]{:T(128)}, f32[24,128,128]{2,1,0:T(8,128)S(1)}, f32[24,128]{1,0:T(8,128)S(1)}, s32[]{:T(128)}, s32[1,1,4,16]{3,2,1,0:T(4,128)S(1)}, /*index=5*...) while((s32[]{:T(128)}, f32[24,128,128]{2,1,0:T(8,128)S(1)}, ...), condition=%wide.region_3.4_spmd, body=%wide.region_2.3_spmd.sunk | while | flops 203167760 | bytes 1594699 | solution.py:100
  102.5 1.4 fusion.122
  103.9 1.0 fusion.123
  112.3 1.4 fusion.122
  122.1 1.4 fusion.122
  132.0 1.4 fusion.122
  141.8 1.4 fusion.122
  151.6 1.4 fusion.122
  161.5 1.4 fusion.122
  162.9 1.0 fusion.123
  171.3 1.4 fusion.122
  172.7 1.0 fusion.123
  181.1 1.4 fusion.122
  191.0 1.4 fusion.122
  200.8 1.4 fusion.122
  202.2 1.0 fusion.123
  210.6 1.4 fusion.122
  220.5 1.4 fusion.122
  221.9 1.0 fusion.123
  223.5 62.1 %collective-permute-start.2 = (f32[512,128]{1,0:T(8,128)}, f32[512,128]{1,0:T(8,128)S(1)}, u32[]{:S(2)}, u32[]{:S(2)}) collective-permute-start(f32[512,128]{1,0:T(8,128)} %collective-permute-done.1), channel_id=1, source_target_pairs={{0,24},{24,48},{48,72},{72,96},{96,120},{120,144},{144,168},{168,1... | collective-permute-start | bytes 786440 | tf_op jit(solution)/shard_map/ppermute | solution.py:17
  285.7 117.2 %while.50 = (s32[]{:T(128)}, f32[24,128,128]{2,1,0:T(8,128)S(1)}, f32[24,128]{1,0:T(8,128)S(1)}, s32[]{:T(128)}, s32[1,1,4,16]{3,2,1,0:T(4,128)S(1)}, /*index=5*...) while((s32[]{:T(128)}, f32[24,128,128]{2,1,0:T(8,128)S(1)}, ...), condition=%wide.region_5.6_spmd, body=%wide.region_4.5_spmd.sunk | while | flops 203167760 | bytes 1594699 | solution.py:100
  292.9 1.4 fusion.130
  302.7 1.4 fusion.130
  312.4 1.4 fusion.130
  322.1 1.4 fusion.130
  331.8 1.4 fusion.130
  333.2 1.0 fusion.131
  341.5 1.4 fusion.130
  342.9 1.0 fusion.131
  351.2 1.4 fusion.130
  360.9 1.4 fusion.130
  362.4 1.0 fusion.131
  370.7 1.4 fusion.130
  380.4 1.4 fusion.130
  390.1 1.4 fusion.130
  399.8 1.4 fusion.130
  402.9 62.7 %while.51 = (s32[]{:T(128)}, f32[24,128,128]{2,1,0:T(8,128)S(1)}, f32[24,128]{1,0:T(8,128)S(1)}, s32[]{:T(128)}, s32[1,1,4,16]{3,2,1,0:T(4,128)S(1)}, /*index=5*...) while((s32[]{:T(128)}, f32[24,128,128]{2,1,0:T(8,128)S(1)}, ...), condition=%wide.region_7.8_spmd, body=%wide.region_6.7_spmd.sunk | while | flops 203167760 | bytes 1594699 | solution.py:100
  465.7 1.1 copy-done
  467.7 203.9 %psum.21 = f32[24,128]{1,0:T(8,128)S(1)} all-reduce(f32[24,128]{1,0:T(8,128)S(1)} %get-tuple-element.207), channel_id=1, replica_groups=mesh['item'=32,'split'=24] {'split'}, use_global_device_ids=true, to_apply=%region_8.9 | all-reduce | flops 3072 | bytes 24576 | tf_op jit(solution)/shard_map/psum | solution.py:102
  671.6 172.4 %all-reduce.3.cloned.1.call-done = f32[24,128,128]{2,1,0:T(8,128)} async-done(((f32[24,128,128]{2,1,0:T(8,128)}), f32[24,128,128]{2,1,0:T(8,128)}) %all-reduce.3.cloned.1.call-update) | async-done | bytes 1572880 | tf_op jit(solution)/shard_map/psum | solution.py:102
  844.0 4.1 fusion.52
  848.5 2.5 fusion.50
  851.5 2.5 fusion.48
  (364 shorter events, 117.4 us)
Async XLA Ops:
  6.5 6.1 copy-start.2
  6.5 6.1 copy-start.3
  6.5 6.1 copy-start.4
  6.5 6.2 copy-start.5
  6.5 6.2 copy-start.6
  6.5 460.3 %all-reduce.5.cloned.1.call-start = ((), (), s32[]{:S(2)}) async-start(), calls=%async_computation.1 | async-start | bytes 131072 | tf_op jit(solution)/shard_map/psum | solution.py:58
  6.6 86.6 %collective-permute-start = (f32[512,128]{1,0:T(8,128)}, f32[512,128]{1,0:T(8,128)}, u32[]{:S(2)}, u32[]{:S(2)}) collective-permute-start(f32[512,128]{1,0:T(8,128)} %param.14), channel_id=1, source_target_pairs={{0,24},{24,48},{48,72},{72,96},{96,120},{120,144},{144,168},{168,1... | collective-permute-start | bytes 786440 | tf_op jit(solution)/shard_map/ppermute | solution.py:17
  11.0 833.1 %all-reduce.3.cloned.1.call-start = ((), (), s32[]{:S(2)}) async-start(), calls=%async_computation | async-start | bytes 3145728 | tf_op jit(solution)/shard_map/psum | solution.py:102
  93.2 130.4 %collective-permute-start.1 = (f32[512,128]{1,0:T(8,128)}, f32[512,128]{1,0:T(8,128)}, u32[]{:S(2)}, u32[]{:S(2)}) collective-permute-start(f32[512,128]{1,0:T(8,128)} %collective-permute-done), channel_id=1, source_target_pairs={{0,24},{24,48},{48,72},{72,96},{96,120},{120,144},{144,168},{168,1... | collective-permute-start | bytes 786440 | tf_op jit(solution)/shard_map/ppermute | solution.py:17
  223.5 179.4 %collective-permute-start.2 = (f32[512,128]{1,0:T(8,128)}, f32[512,128]{1,0:T(8,128)S(1)}, u32[]{:S(2)}, u32[]{:S(2)}) collective-permute-start(f32[512,128]{1,0:T(8,128)} %collective-permute-done.1), channel_id=1, source_target_pairs={{0,24},{24,48},{48,72},{72,96},{96,120},{120,144},{144,168},{168,1... | collective-permute-start | bytes 786440 | tf_op jit(solution)/shard_map/ppermute | solution.py:17
  465.6 1.2 copy-start
  844.0 4.5 copy-start.1
Sparse Core Ops, SparseCore 0:
  11.1 250.0 all-reduce.4
  466.9 377.0 all-reduce.2
where the time goes:
time: 879 us; the launch traced here: 862 us
  loops' own time  231 us (26%)
  blocking collectives  204 us (23%)
  waiting for transfers between devices  173 us (20%)
  matrix products  86.5 us (10%)
  starting transfers between devices  66.2 us (8%)
  other arithmetic  59.7 us (7%)
  local copies, waits for them, and re-layouts  28.4 us (3%)
  between operations  13.6 us (2%)
    another operation x4, loops' own time, body(): carried = lax.fori_loop(0, block_count[0, 0, loop_step], add_block, carried)  231 us
    psum x1, blocking collectives, body(): summed_gram, summed_right = lax.psum((user_gram, user_right), 'split')  204 us
    psum x1, waiting for transfers between devices, body(): summed_gram, summed_right = lax.psum((user_gram, user_right), 'split')  172 us
    ppermute x3, starting transfers between devices, shifted(): return lax.ppermute(value, axis, pairs)  66.1 us
    dot_general x45, matrix products, add_block(): jnp.dot(weighted.reshape(block_users * features, block_items), item_rows,...  46.7 us
    mul x45, other arithmetic, block_parts(): user_start = user_block[0, 0, loop_step, position] * block_users  28.7 us
    dot_general x45, matrix products, add_block(): jnp.dot(weights + recency, item_rows, precision=lax.Precision.HIGHEST, pr...  28.4 us
    convert_element_type x45, other arithmetic, block_parts(): block_age[0, 0, loop_step, position].astype(jnp.float32)  27.9 us
  transfers between devices with their start and end apart: 5, of which 1 were waited for; matrix products, arithmetic and copies ran while one was open for 19% of the time, Pallas kernels for 0%

commit v1 on v0

v1 whole, which is shorter than its diff:
```python
import jax
import jax.numpy as jnp
from jax import lax
from jax.experimental import pallas as pl
from jax.experimental.pallas import tpu as pltpu
from jax.sharding import PartitionSpec as P

CG_ITERS = 3
STEPS = 4
SLOTS = 16
USERS = 24
EMB = 128
ROWS = 512
X, Y, C = 4, 4, 2
N_ITEM = X * Y * C
Z = 12
N_SPLIT = 2 * Z
NEAR = Y * C
CHUNKS = 2
CHUNK = ROWS // CHUNKS
RIDGE = 0.1
F32 = jnp.float32
BF16 = jnp.bfloat16
MESH = pl.DeviceIdType.MESH


def high_low(value):
    high = value.astype(BF16)
    return high, (value - high.astype(F32)).astype(BF16)


def block_weights(user_block, item_block, block_age, block_count):
    lane = lax.broadcasted_iota(jnp.int32, (STEPS, SLOTS), 1)
    row = lax.broadcasted_iota(jnp.int32, (STEPS, STEPS), 0)
    col = lax.broadcasted_iota(jnp.int32, (STEPS, STEPS), 1)
    counts = jnp.broadcast_to(block_count.astype(F32), (STEPS, STEPS))
    counts = jnp.sum(jnp.where(row == col, counts, 0.0), axis=1, keepdims=True)
    recency = 2.0 / (2.0 + block_age.astype(F32))
    recency = jnp.where(lane.astype(F32) < counts, recency, 0.0)
    code = (user_block * 4 + item_block).astype(F32)
    both = jnp.concatenate([recency, code], axis=0)
    slot = lax.broadcasted_iota(jnp.int32, (SLOTS, EMB), 0)
    spread = lax.broadcasted_iota(jnp.int32, (SLOTS, EMB), 1) // 8
    spread = jnp.where(slot == spread, 1.0, 0.0).astype(F32)
    return jnp.dot(both, spread, precision=lax.Precision.HIGHEST, preferred_element_type=F32)


def kernel(
    emb_ref, conf_ref, user_ref, item_ref, age_ref, count_ref, out_ref,
    send_a, recv_a, send_r, recv_r, pair_c, pair_r, recv_b, recv_s,
    window, window_t, split_w, local_gram, gram_1, gram_2, gram_3, result,
    sem_as, sem_ar, sem_rs, sem_rr, sem_bs, sem_br,
    sem_ws, sem_wr, sem_g1s, sem_g1r, sem_g2s, sem_g2r, sem_g3s, sem_g3r,
    sem_xs, sem_xr,
):
    item = lax.axis_index("item")
    split = lax.axis_index("split")
    core = lax.rem(item, C)
    near = lax.rem(item, NEAR)
    at_x = item // NEAR
    at_y = near // C
    y_hi = split // Z
    at_z = lax.rem(split, Z)
    other_y = 1 - y_hi
    partner = other_y * Z + at_z
    user = 2 * at_z + y_hi
    last_y = (at_y == Y - 1).astype(jnp.int32)
    first_y = (at_y == 0).astype(jnp.int32)
    next_split = (y_hi + last_y * (1 - 2 * y_hi)) * Z + at_z
    prev_split = (y_hi + first_y * (1 - 2 * y_hi)) * Z + at_z
    next_item = lax.rem(item + C, N_ITEM)
    prev_item = lax.rem(item + N_ITEM - C, N_ITEM)
    other_core = item + 1 - 2 * core

    def at_split(d):
        return lax.rem(split + d, N_SPLIT)

    def at_depth(d):
        return lax.rem(at_z + d, Z)

    def at_near(d):
        return lax.rem(near + d, NEAR)

    def at_far(d):
        return lax.rem(at_x + d, X)

    barrier = pltpu.get_barrier_semaphore()

    def greet(device):
        pl.semaphore_signal(barrier, inc=1, device_id=device, device_id_type=MESH)

    @pl.loop(1, N_SPLIT)
    def _(d):
        greet((item, at_split(d)))

    @pl.loop(1, NEAR)
    def _(d):
        greet((at_x * NEAR + at_near(d), split))

    @pl.loop(1, X)
    def _(d):
        greet((at_far(d) * NEAR + near, split))

    greet((next_item, next_split))
    greet((prev_item, prev_split))

    @pl.when(core == 1)
    def _():
        greet((lax.rem(item + 1, N_ITEM), next_split))

    @pl.when(core == 0)
    def _():
        greet((lax.rem(item + N_ITEM - 1, N_ITEM), prev_split))

    def copy(src, dst, send_sem, recv_sem, device):
        return pltpu.make_async_remote_copy(
            src_ref=src, dst_ref=dst, send_sem=send_sem, recv_sem=recv_sem,
            device_id=device, device_id_type=MESH,
        )

    spread = block_weights(user_ref[...], item_ref[...], age_ref[...], count_ref[...])
    half = USERS * 8
    row = lax.broadcasted_iota(jnp.int32, (half, 1), 0)
    row_user = row // 8
    row_code = ((row_user // 8) * 4 + lax.rem(row, 4)) * 16
    row_code = row_code + (lax.rem(row, 8) // 4) * 8 + lax.rem(row_user, 8)
    row_code = row_code.astype(F32)
    lane = lax.broadcasted_iota(jnp.int32, (1, 2 * EMB), 1)
    lane_code = (lane // EMB * 8 + lax.rem(lane, 8)).astype(F32)
    ones = jnp.ones((2 * EMB, EMB), BF16)
    rows_8 = lax.broadcasted_iota(jnp.int32, (8, EMB), 0)
    lanes_8 = lax.broadcasted_iota(jnp.int32, (8, EMB), 1)
    recency_rows = [jnp.zeros((1, EMB), F32) for _ in range(3)]
    for pair in range(2):
        k = 2 * pair
        recency = jnp.concatenate([spread[k : k + 1], spread[k + 1 : k + 2]], axis=1)
        code = jnp.concatenate([spread[4 + k : 5 + k], spread[5 + k : 6 + k]], axis=1)
        code = code * 16.0 + lane_code
        place = jnp.where(row_code == code, recency, 0.0)
        high, rest = high_low(place)
        low = (place - high.astype(F32) - rest.astype(F32)).astype(BF16)
        values = jnp.concatenate([conf_ref[pl.ds(2 * EMB * pair, 2 * EMB), :], ones], axis=1)
        sums = jnp.dot(
            jnp.concatenate([high, rest, low], axis=0), values, preferred_element_type=F32
        )
        sums = sums[:half] + sums[half : 2 * half] + sums[2 * half :]
        send_a[:, pl.ds(8 * pair, 8), :] = sums[:, :EMB].reshape(USERS, 8, EMB)
        for block in range(3):
            part = sums[64 * block : 64 * block + 8, EMB:]
            part = jnp.where(lanes_8 == rows_8 + 8 * pair, part, 0.0)
            recency_rows[block] = recency_rows[block] + jnp.sum(part, axis=0, keepdims=True)
    for block in range(3):
        send_r[block] = recency_rows[block]

    pl.semaphore_wait(barrier, N_SPLIT - 1 + NEAR - 1 + X - 1 + 3)

    def own_next(c):
        return copy(
            emb_ref.at[pl.ds(c * CHUNK, CHUNK)], window.at[2, pl.ds(c * CHUNK, CHUNK)],
            sem_ws.at[0, c], sem_wr.at[1, c], (next_item, next_split),
        )

    def own_core(c):
        return copy(
            emb_ref.at[pl.ds(c * CHUNK, CHUNK)], window.at[1, pl.ds(c * CHUNK, CHUNK)],
            sem_ws.at[1, c], sem_wr.at[0, c], (other_core, split),
        )

    def relay_core(c, slot, send_slot):
        return copy(
            window.at[2, pl.ds(c * CHUNK, CHUNK)], window.at[slot, pl.ds(c * CHUNK, CHUNK)],
            sem_ws.at[send_slot, c], sem_wr.at[slot - 1, c], (other_core, split),
        )

    def relay_next(c):
        return copy(
            window.at[2, pl.ds(c * CHUNK, CHUNK)], window.at[3, pl.ds(c * CHUNK, CHUNK)],
            sem_ws.at[2, c], sem_wr.at[2, c], (lax.rem(item + 1, N_ITEM), next_split),
        )

    for c in range(CHUNKS):
        own_next(c).start()

    def depth_copy(d):
        peer = at_depth(d)
        return copy(
            send_a.at[pl.ds(2 * peer, 2)], recv_a.at[at_z],
            sem_as.at[d], sem_ar.at[at_z], (item, y_hi * Z + peer),
        )

    def depth_copy_r(d):
        peer = at_depth(d)
        return copy(
            send_r.at[peer // 4], recv_r.at[at_z],
            sem_rs.at[d], sem_rr.at[at_z], (item, y_hi * Z + peer),
        )

    @pl.loop(1, Z)
    def _(d):
        depth_copy(d).start()
        depth_copy_r(d).start()

    @pl.when(core == 0)
    def _():
        for c in range(CHUNKS):
            own_core(c).start()

    def prepare(slot, rows):
        high, low = high_low(rows)
        split_w[slot, :, pl.ds(0, EMB)] = high
        split_w[slot, :, pl.ds(EMB, EMB)] = low
        turned = rows.T
        window_t[slot] = turned
        return turned

    def three_products(left, slot):
        high, low = high_low(left)
        count = left.shape[0]
        both = jnp.concatenate([high, low], axis=0)
        out = jnp.dot(both, split_w[slot], preferred_element_type=F32)
        return out[:count, :EMB] + out[:count, EMB:] + out[count:, :EMB]

    turned = prepare(0, emb_ref[...])
    local_gram[...] = three_products(turned, 0).reshape(NEAR, EMB // NEAR, EMB)

    def gram_copy_1(d):
        peer = at_near(d)
        return copy(
            local_gram.at[peer], gram_1.at[near],
            sem_g1s.at[d], sem_g1r.at[near], (at_x * NEAR + peer, split),
        )

    def gram_copy_2(d):
        peer = at_far(d)
        return copy(
            gram_2.at[at_x], gram_2.at[at_x],
            sem_g2s.at[d], sem_g2r.at[at_x], (peer * NEAR + near, split),
        )

    def gram_copy_3(d):
        peer = at_near(d)
        return copy(
            gram_3.at[near], gram_3.at[near],
            sem_g3s.at[d], sem_g3r.at[near], (at_x * NEAR + peer, split),
        )

    @pl.loop(1, NEAR)
    def _(d):
        gram_copy_1(d).start()

    for c in range(CHUNKS):
        own_next(c).wait_recv()

        @pl.when(core == 0)
        def _():
            relay_core(c, 3, 2).start()

        @pl.when(core == 1)
        def _():
            relay_next(c).start()
            relay_core(c, 1, 1).start()

    def sum_1(d, total):
        peer = at_near(d)
        copy(
            local_gram.at[peer], gram_1.at[peer], sem_g1s.at[d], sem_g1r.at[peer],
            (at_x * NEAR + peer, split),
        ).wait_recv()
        return total + gram_1[peer]

    gram_2[at_x] = lax.fori_loop(1, NEAR, sum_1, local_gram[near])

    @pl.loop(1, X)
    def _(d):
        gram_copy_2(d).start()

    def sum_z(d, totals):
        total, total_r = totals
        peer = at_depth(d)
        copy(
            send_a.at[pl.ds(0, 2)], recv_a.at[peer], sem_as.at[d], sem_ar.at[peer],
            (item, y_hi * Z + peer),
        ).wait_recv()
        copy(
            send_r.at[0], recv_r.at[peer], sem_rs.at[d], sem_rr.at[peer],
            (item, y_hi * Z + peer),
        ).wait_recv()
        return total + recv_a[peer], total_r + recv_r[peer]

    total, total_r = lax.fori_loop(
        1, Z, sum_z, (send_a[pl.ds(2 * at_z, 2)], send_r[at_z // 4])
    )
    pair_c[...] = total
    pair_r[...] = total_r
    send_pair = copy(
        pair_c.at[other_y], recv_b, sem_bs.at[0], sem_br.at[0], (item, partner)
    )
    send_pair_r = copy(pair_r, recv_s, sem_bs.at[1], sem_br.at[1], (item, partner))
    send_pair.start()
    send_pair_r.start()

    def sum_2(d, total):
        peer = at_far(d)
        copy(
            gram_2.at[peer], gram_2.at[peer], sem_g2s.at[d], sem_g2r.at[peer],
            (peer * NEAR + near, split),
        ).wait_recv()
        return total + gram_2[peer]

    gram_3[near] = lax.fori_loop(1, X, sum_2, gram_2[at_x])

    @pl.loop(1, NEAR)
    def _(d):
        gram_copy_3(d).start()

    prepare(2, window[2])
    send_pair.wait_recv()
    send_pair_r.wait_recv()
    weights = pair_c[y_hi] + recv_b[...]
    block_row = jnp.broadcast_to(pair_r[...] + recv_s[...], (SLOTS, EMB))
    rows_16 = lax.broadcasted_iota(jnp.int32, (SLOTS, EMB), 0)
    lanes_16 = lax.broadcasted_iota(jnp.int32, (SLOTS, EMB), 1)
    block_col = jnp.sum(jnp.where(rows_16 == lanes_16, block_row, 0.0), axis=1, keepdims=True)
    wishes = weights + block_col

    def weighted(slot):
        base = 4 * slot
        left = jnp.concatenate(
            [
                window_t[slot, :, pl.ds(b * EMB, EMB)] * weights[base + b : base + b + 1]
                for b in range(4)
            ],
            axis=1,
        )
        wish = jnp.concatenate([wishes[base + b : base + b + 1] for b in range(4)], axis=1)
        wish = jnp.broadcast_to(wish, (8, ROWS))
        return three_products(jnp.concatenate([left, wish], axis=0), slot)

    system = weighted(0) + weighted(2)
    for slot in (1, 3):
        for c in range(CHUNKS):
            copy(
                window.at[2, pl.ds(c * CHUNK, CHUNK)],
                window.at[slot, pl.ds(c * CHUNK, CHUNK)],
                sem_ws.at[0, c], sem_wr.at[slot - 1, c], (other_core, split),
            ).wait_recv()
        prepare(slot, window[slot])
        system = system + weighted(slot)

    @pl.loop(1, NEAR)
    def _(d):
        peer = at_near(d)
        copy(
            gram_3.at[peer], gram_3.at[peer], sem_g3s.at[d], sem_g3r.at[peer],
            (at_x * NEAR + peer, split),
        ).wait_recv()

    eye = lax.broadcasted_iota(jnp.int32, (EMB, EMB), 0)
    eye = eye == lax.broadcasted_iota(jnp.int32, (EMB, EMB), 1)
    base = gram_3[...].reshape(EMB, EMB) + jnp.where(eye, RIDGE, 0.0)
    matrix = system[:EMB] + base
    right = system[EMB:]

    def over(value):
        return jnp.sum(value, axis=1, keepdims=True)

    answer = jnp.zeros_like(right)
    residual = right
    direction = right
    norm_now = over(residual * residual)
    for _ in range(CG_ITERS):
        image = jnp.dot(
            direction, matrix, precision=lax.Precision.HIGHEST, preferred_element_type=F32
        )
        step_size = norm_now / over(direction * image)
        answer = answer + step_size * direction
        residual = residual - step_size * image
        norm_next = over(residual * residual)
        direction = residual + (norm_next / norm_now) * direction
        norm_now = norm_next
    result[user] = answer[:1]

    def answer_copy(d):
        return copy(
            result.at[user], result.at[user], sem_xs.at[d], sem_xr.at[split],
            (item, at_split(d)),
        )

    @pl.loop(1, N_SPLIT)
    def _(d):
        answer_copy(d).start()

    for c in range(CHUNKS):
        own_next(c).wait_send()
        relay_core(c, 1, 1).wait_send()
        relay_next(c).wait_send()

    @pl.loop(1, Z)
    def _(d):
        depth_copy(d).wait_send()
        depth_copy_r(d).wait_send()

    send_pair.wait_send()
    send_pair_r.wait_send()

    @pl.loop(1, NEAR)
    def _(d):
        gram_copy_1(d).wait_send()
        gram_copy_3(d).wait_send()

    @pl.loop(1, X)
    def _(d):
        gram_copy_2(d).wait_send()

    @pl.loop(1, N_SPLIT)
    def _(d):
        peer = at_split(d)
        row = 2 * lax.rem(peer, Z) + peer // Z
        copy(
            result.at[row], result.at[row], sem_xs.at[d], sem_xr.at[peer], (item, peer)
        ).wait_recv()

    @pl.loop(1, N_SPLIT)
    def _(d):
        answer_copy(d).wait_send()

    for u in range(USERS):
        out_ref[u : u + 1, :] = result[u]


def body(item_emb, confidences, user_block, item_block, block_age, block_count):
    dma = pltpu.SemaphoreType.DMA
    vmem = pl.BlockSpec(memory_space=pltpu.VMEM)
    return pl.pallas_call(
        kernel,
        out_shape=jax.ShapeDtypeStruct((USERS, EMB), F32),
        in_specs=[vmem] * 6,
        out_specs=vmem,
        scratch_shapes=[
            pltpu.VMEM((USERS, SLOTS, EMB), F32),
            pltpu.VMEM((Z, 2, SLOTS, EMB), F32),
            pltpu.VMEM((3, 1, EMB), F32),
            pltpu.VMEM((Z, 1, EMB), F32),
            pltpu.VMEM((2, SLOTS, EMB), F32),
            pltpu.VMEM((1, EMB), F32),
            pltpu.VMEM((SLOTS, EMB), F32),
            pltpu.VMEM((1, EMB), F32),
            pltpu.VMEM((STEPS, ROWS, EMB), F32),
            pltpu.VMEM((STEPS, EMB, ROWS), F32),
            pltpu.VMEM((STEPS, ROWS, 2 * EMB), BF16),
            pltpu.VMEM((NEAR, EMB // NEAR, EMB), F32),
            pltpu.VMEM((NEAR, EMB // NEAR, EMB), F32),
            pltpu.VMEM((X, EMB // NEAR, EMB), F32),
            pltpu.VMEM((NEAR, EMB // NEAR, EMB), F32),
            pltpu.VMEM((USERS, 1, EMB), F32),
            dma((Z,)), dma((Z,)), dma((Z,)), dma((Z,)), dma((2,)), dma((2,)),
            dma((3, CHUNKS)), dma((3, CHUNKS)),
            dma((NEAR,)), dma((NEAR,)), dma((X,)), dma((X,)), dma((NEAR,)), dma((NEAR,)),
            dma((N_SPLIT,)), dma((N_SPLIT,)),
        ],
        compiler_params=pltpu.CompilerParams(
            collective_id=0, has_side_effects=True, vmem_limit_bytes=32 << 20
        ),
        name="als_half_sweep",
    )(
        item_emb,
        confidences.reshape(ROWS, EMB),
        user_block.reshape(STEPS, SLOTS),
        item_block.reshape(STEPS, SLOTS),
        block_age.reshape(STEPS, SLOTS),
        block_count.reshape(1, STEPS),
    )


def solution(mesh):
    placed = (
        P("item", None),
        P("item", "split", None, None, None, None),
        P("item", "split", None, None),
        P("item", "split", None, None),
        P("item", "split", None, None),
        P("item", "split", None),
    )
    return jax.shard_map(
        body, mesh=mesh, in_specs=placed, out_specs=P("item", None), check_vma=False
    )
```

time: 879 us -> 51.3 us (0.06)
  the two profiles are of different devices: /device:TPU:6 before, /device:TPU:1 now
where the time goes in v1:
time: 51.3 us; the launch traced here: 51.1 us
  Pallas kernels  47.9 us (93%)
  local copies, waits for them, and re-layouts  3.16 us (6%)
    pallas_call x1, Pallas kernels, body(): pl.pallas_call(kernel, out_shape=jax.ShapeDtypeStruct((USERS, EMB), F32),...  47.9 us
    unnamed x13, local copies, waits for them, and re-layouts  3.16 us

profile of v1, /device:TPU:1, one launch (start us, length us, event | category | flops | bytes accessed | tf_op | source)
XLA Modules:
  0.0 51.1 jit_solution(1319818500209620336)
XLA Ops:
  0.0 0.0 copy-start.4
  0.0 0.0 copy-start.3
  0.0 0.0 copy-start.2
  0.0 0.0 copy-start.5
  0.0 0.7 %copy-done.4 = s32[1,1,4,16]{3,2,1,0:T(4,128)S(1)} copy-done((s32[1,1,4,16]{3,2,1,0:T(4,128)S(1)}, s32[1,1,4,16]{3,2,1,0:T(4,128)}, u32[]{:S(2)}) %copy-start.4) | copy-done | bytes 280
  0.7 0.0 copy-done.3
  0.7 0.0 copy-done.2
  0.7 0.0 copy-done.5
  0.7 0.0 copy-start
  0.7 0.9 %copy-done = f32[512,128]{1,0:T(8,128)S(1)} copy-done((f32[512,128]{1,0:T(8,128)S(1)}, f32[512,128]{1,0:T(8,128)}, u32[]{:S(2)}) %copy-start) | copy-done | bytes 262168
  1.7 0.0 copy-start.1
  1.7 0.9 %copy-done.1 = bf16[1,1,4,16,8,128]{5,4,3,2,1,0:T(8,128)(2,1)S(1)} copy-done((bf16[1,1,4,16,8,128]{5,4,3,2,1,0:T(8,128)(2,1)S(1)}, bf16[1,1,4,16,8,128]{5,4,3,2,1,0:T(8,128)(2,1)}, u32[]{:S(2)}) %copy-start.1) | copy-done | bytes 131096
  2.6 47.9 %als_half_sweep.1 = f32[24,128]{1,0:T(8,128)S(1)} custom-call(f32[512,128]{1,0:T(8,128)S(1)} %copy-done, bf16[512,128]{1,0:T(8,128)(2,1)S(1)} %bitcast.5, s32[4,16]{1,0:T(4,128)S(1)} %bitcast.6, s32[4,16]{1,0:T(4,128)S(1)} %bitcast.7, s32[4,16]{1,0:T(4,128)S(1)} %bitcast.8, s32[1,4]{1,0:T(1,128)S(1)} %bitcast.9), custom_call_target="tpu_custom_call" | custom-call | tf_op jit(solution)/shard_map/als_half_sweep/pallas_call | solution.py:434
  50.5 0.6 %copy.8 = f32[24,128]{1,0:T(8,128)} copy(f32[24,128]{1,0:T(8,128)S(1)} %als_half_sweep.1) | data formatting | bytes 24576
Async XLA Ops:
  0.0 0.7 %copy-start.4 = (s32[1,1,4,16]{3,2,1,0:T(4,128)S(1)}, s32[1,1,4,16]{3,2,1,0:T(4,128)}, u32[]{:S(2)}) copy-start(s32[1,1,4,16]{3,2,1,0:T(4,128)} %param.10) | copy-start | bytes 772
  0.0 0.7 %copy-start.3 = (s32[1,1,4,16]{3,2,1,0:T(4,128)S(1)}, s32[1,1,4,16]{3,2,1,0:T(4,128)}, u32[]{:S(2)}) copy-start(s32[1,1,4,16]{3,2,1,0:T(4,128)} %param.9) | copy-start | bytes 772
  0.0 0.7 %copy-start.2 = (s32[1,1,4,16]{3,2,1,0:T(4,128)S(1)}, s32[1,1,4,16]{3,2,1,0:T(4,128)}, u32[]{:S(2)}) copy-start(s32[1,1,4,16]{3,2,1,0:T(4,128)} %param.8) | copy-start | bytes 772
  0.0 0.7 %copy-start.5 = (s32[1,1,4]{2,1,0:T(1,128)S(1)}, s32[1,1,4]{2,1,0:T(1,128)}, u32[]{:S(2)}) copy-start(s32[1,1,4]{2,1,0:T(1,128)} %param.11) | copy-start | bytes 52
  0.7 1.0 %copy-start = (f32[512,128]{1,0:T(8,128)S(1)}, f32[512,128]{1,0:T(8,128)}, u32[]{:S(2)}) copy-start(f32[512,128]{1,0:T(8,128)} %emb_ref.1) | copy-start | bytes 786436
  1.7 0.9 %copy-start.1 = (bf16[1,1,4,16,8,128]{5,4,3,2,1,0:T(8,128)(2,1)S(1)}, bf16[1,1,4,16,8,128]{5,4,3,2,1,0:T(8,128)(2,1)}, u32[]{:S(2)}) copy-start(bf16[1,1,4,16,8,128]{5,4,3,2,1,0:T(8,128)(2,1)} %param.7) | copy-start | bytes 393220

commit v2 on v1

v2 whole, which is shorter than its diff:
```python
import jax
import jax.numpy as jnp
from jax import lax
from jax.experimental import pallas as pl
from jax.experimental.pallas import tpu as pltpu
from jax.sharding import PartitionSpec as P

CG_ITERS = 3
STEPS = 4
SLOTS = 16
USERS = 24
EMB = 128
ROWS = 512
X, Y, C = 4, 4, 2
N_ITEM = X * Y * C
Z = 12
SIDE = X * C
BLOCK = EMB // SIDE
CHUNKS = 2
CHUNK = ROWS // CHUNKS
RIDGE = 0.1
HELD = 40
SENT = 33
FAR_FIRST = (6, 5, 7, 4, 8, 3, 9, 2, 10, 1, 11)
F32 = jnp.float32
BF16 = jnp.bfloat16
MESH = pl.DeviceIdType.MESH


def high_low(value):
    high = value.astype(BF16)
    return high, (value - high.astype(F32)).astype(BF16)


def block_weights(user_block, item_block, block_age, block_count):
    lane = lax.broadcasted_iota(jnp.int32, (STEPS, SLOTS), 1)
    row = lax.broadcasted_iota(jnp.int32, (STEPS, STEPS), 0)
    col = lax.broadcasted_iota(jnp.int32, (STEPS, STEPS), 1)
    counts = jnp.broadcast_to(block_count.astype(F32), (STEPS, STEPS))
    counts = jnp.sum(jnp.where(row == col, counts, 0.0), axis=1, keepdims=True)
    recency = 2.0 / (2.0 + block_age.astype(F32))
    recency = jnp.where(lane.astype(F32) < counts, recency, 0.0)
    code = (user_block * 4 + item_block).astype(F32)
    both = jnp.concatenate([recency, code], axis=0)
    slot = lax.broadcasted_iota(jnp.int32, (SLOTS, EMB), 0)
    spread = lax.broadcasted_iota(jnp.int32, (SLOTS, EMB), 1) // 8
    spread = jnp.where(slot == spread, 1.0, 0.0).astype(F32)
    return jnp.dot(both, spread, precision=lax.Precision.HIGHEST, preferred_element_type=F32)


def kernel(
    emb_hbm, conf_hbm, user_hbm, item_hbm, age_hbm, count_hbm, out_ref,
    emb_ref, conf_ref, user_ref, item_ref, age_ref, count_ref,
    send_a, recv_a, pair_a, recv_b,
    window, window_t, split_w, local_gram, gram_1, gram_2, gram_3, result,
    sem_in, sem_as, sem_ar, sem_bs, sem_br,
    sem_ws, sem_wr, sem_g1s, sem_g1r, sem_g2s, sem_g2r, sem_g3s, sem_g3r,
    sem_xs, sem_xr,
):
    item = lax.axis_index("item")
    split = lax.axis_index("split")
    core = lax.rem(item, C)
    at_x = item // (Y * C)
    at_y = lax.rem(item, Y * C) // C
    side = at_x * C + core
    y_hi = split // Z
    at_z = lax.rem(split, Z)
    partner = (1 - y_hi) * Z + at_z
    last_y = (at_y == Y - 1).astype(jnp.int32)
    first_y = (at_y == 0).astype(jnp.int32)
    next_split = (y_hi + last_y * (1 - 2 * y_hi)) * Z + at_z
    prev_split = (y_hi + first_y * (1 - 2 * y_hi)) * Z + at_z
    next_item = lax.rem(item + C, N_ITEM)
    prev_item = lax.rem(item + N_ITEM - C, N_ITEM)
    cross_next = lax.rem(item + 1, N_ITEM)
    cross_prev = lax.rem(item + N_ITEM - 1, N_ITEM)
    other_core = item + 1 - 2 * core

    def at_depth(d):
        return lax.rem(at_z + d, Z)

    def at_side(d):
        peer = lax.rem(side + d, SIDE)
        return peer, (peer // C * (Y * C) + at_y * C + lax.rem(peer, C), split)

    def along_y(d):
        place = lax.rem(y_hi * Y + at_y + d + 2 * Y, 2 * Y)
        at = lax.rem(place, Y)
        return at, (at_x * (Y * C) + at * C + core, place // Y * Z + at_z)

    barrier = pltpu.get_barrier_semaphore()

    def greet(device):
        pl.semaphore_signal(barrier, inc=1, device_id=device, device_id_type=MESH)

    for d in FAR_FIRST:
        greet((item, y_hi * Z + at_depth(d)))
    greet((item, partner))
    for d in (1, 2, 3, -1, -2, -3):
        greet(along_y(d)[1])
    for d in range(1, SIDE):
        greet(at_side(d)[1])
    greet((next_item, next_split))
    greet((prev_item, prev_split))

    @pl.when(core == 1)
    def _():
        greet((cross_next, next_split))

    @pl.when(core == 0)
    def _():
        greet((cross_prev, prev_split))

    loads = [
        pltpu.make_async_copy(src, dst, sem_in.at[n])
        for n, (src, dst) in enumerate(
            (
                (user_hbm, user_ref),
                (item_hbm, item_ref),
                (age_hbm, age_ref),
                (count_hbm, count_ref),
                (conf_hbm, conf_ref),
                (emb_hbm, emb_ref),
            )
        )
    ]
    for load in loads:
        load.start()

    def copy(src, dst, send_sem, recv_sem, device):
        return pltpu.make_async_remote_copy(
            src_ref=src, dst_ref=dst, send_sem=send_sem, recv_sem=recv_sem,
            device_id=device, device_id_type=MESH,
        )

    for load in loads[:4]:
        load.wait()
    spread = block_weights(user_ref[...], item_ref[...], age_ref[...], count_ref[...])
    half = USERS * 8
    row = lax.broadcasted_iota(jnp.int32, (half, 1), 0)
    row_user = row // 8
    row_code = ((row_user // 8) * 4 + lax.rem(row, 4)) * 16
    row_code = row_code + (lax.rem(row, 8) // 4) * 8 + lax.rem(row_user, 8)
    row_code = row_code.astype(F32)
    lane = lax.broadcasted_iota(jnp.int32, (1, 2 * EMB), 1)
    lane_code = (lane // EMB * 8 + lax.rem(lane, 8)).astype(F32)
    ones = jnp.ones((2 * EMB, EMB), BF16)
    rows_8 = lax.broadcasted_iota(jnp.int32, (8, EMB), 0)
    lanes_8 = lax.broadcasted_iota(jnp.int32, (8, EMB), 1)
    recency_rows = [jnp.zeros((1, EMB), F32) for _ in range(3)]
    loads[4].wait()
    for pair in range(2):
        k = 2 * pair
        recency = jnp.concatenate([spread[k : k + 1], spread[k + 1 : k + 2]], axis=1)
        code = jnp.concatenate([spread[4 + k : 5 + k], spread[5 + k : 6 + k]], axis=1)
        code = code * 16.0 + lane_code
        place = jnp.where(row_code == code, recency, 0.0)
        high, rest = high_low(place)
        low = (place - high.astype(F32) - rest.astype(F32)).astype(BF16)
        values = jnp.concatenate([conf_ref[pl.ds(2 * EMB * pair, 2 * EMB), :], ones], axis=1)
        sums = jnp.dot(
            jnp.concatenate([high, rest, low], axis=0), values, preferred_element_type=F32
        )
        sums = sums[:half] + sums[half : 2 * half] + sums[2 * half :]
        by_user = sums[:, :EMB].reshape(Z, 2, 8, EMB)
        for u in range(2):
            send_a[:, pl.ds(SLOTS * u + 8 * pair, 8), :] = by_user[:, u]
        for block in range(3):
            part = sums[64 * block : 64 * block + 8, EMB:]
            part = jnp.where(lanes_8 == rows_8 + 8 * pair, part, 0.0)
            recency_rows[block] = recency_rows[block] + jnp.sum(part, axis=0, keepdims=True)
    for peer in range(Z):
        send_a[peer, 2 * SLOTS : 2 * SLOTS + 1, :] = recency_rows[peer // 4]

    def prepare(slot, rows):
        high, low = high_low(rows)
        split_w[slot, :, pl.ds(0, EMB)] = high
        split_w[slot, :, pl.ds(EMB, EMB)] = low
        turned = rows.T
        window_t[slot] = turned
        return turned

    def three_products(left, slot):
        high, low = high_low(left)
        count = left.shape[0]
        both = jnp.concatenate([high, low], axis=0)
        out = jnp.dot(both, split_w[slot], preferred_element_type=F32)
        return out[:count, :EMB] + out[:count, EMB:] + out[count:, :EMB]

    loads[5].wait()
    turned = prepare(0, emb_ref[...])
    local_gram[...] = three_products(turned, 0).reshape(SIDE, BLOCK, EMB)

    pl.semaphore_wait(barrier, Z - 1 + 1 + 6 + SIDE - 1 + 3)

    def chunk(c):
        return pl.ds(c * CHUNK, CHUNK)

    def own_next(c):
        return copy(
            emb_ref.at[chunk(c)], window.at[2, chunk(c)],
            sem_ws.at[0, c], sem_wr.at[1, c], (next_item, next_split),
        )

    def own_core(c):
        return copy(
            emb_ref.at[chunk(c)], window.at[1, chunk(c)],
            sem_ws.at[1, c], sem_wr.at[0, c], (other_core, split),
        )

    def relay_core(c, slot, send_slot):
        return copy(
            window.at[2, chunk(c)], window.at[slot, chunk(c)],
            sem_ws.at[send_slot, c], sem_wr.at[slot - 1, c], (other_core, split),
        )

    def relay_next(c):
        return copy(
            window.at[2, chunk(c)], window.at[3, chunk(c)],
            sem_ws.at[2, c], sem_wr.at[2, c], (cross_next, next_split),
        )

    def pass_on(c):
        own_next(c).wait_recv()

        @pl.when(core == 1)
        def _():
            relay_next(c).start()

    def share(c):
        @pl.when(core == 0)
        def _():
            relay_core(c, 3, 2).start()

        @pl.when(core == 1)
        def _():
            relay_core(c, 1, 1).start()

    def depth_copy(d):
        peer = at_depth(d)
        return copy(
            send_a.at[peer, pl.ds(0, SENT)], recv_a.at[at_z, pl.ds(0, SENT)],
            sem_as.at[d], sem_ar.at[at_z], (item, y_hi * Z + peer),
        )

    def gram_copy_1(d):
        peer, device = at_side(d)
        return copy(
            local_gram.at[peer], gram_1.at[side], sem_g1s.at[d], sem_g1r.at[side], device
        )

    def gram_copy_2(n, d):
        return copy(
            gram_2.at[at_y], gram_2.at[at_y], sem_g2s.at[n], sem_g2r.at[at_y], along_y(d)[1]
        )

    def gram_copy_3(d):
        return copy(
            gram_3.at[side], gram_3.at[side], sem_g3s.at[d], sem_g3r.at[side], at_side(d)[1]
        )

    for d in FAR_FIRST:
        depth_copy(d).start()
    for d in range(1, SIDE):
        gram_copy_1(d).start()
    for c in range(CHUNKS):
        own_next(c).start()

    @pl.when(core == 0)
    def _():
        for c in range(CHUNKS):
            own_core(c).start()

    def sum_z(d, total):
        peer = at_depth(d)
        copy(
            send_a.at[0, pl.ds(0, SENT)], recv_a.at[peer, pl.ds(0, SENT)],
            sem_as.at[d], sem_ar.at[peer], (item, y_hi * Z + peer),
        ).wait_recv()
        return total + recv_a[peer, pl.ds(0, SENT)]

    pair_a[pl.ds(0, SENT)] = lax.fori_loop(1, Z, sum_z, send_a[at_z, pl.ds(0, SENT)])
    send_pair = copy(
        pair_a.at[pl.ds(0, SENT)], recv_b.at[pl.ds(0, SENT)], sem_bs, sem_br, (item, partner)
    )
    send_pair.start()

    total = local_gram[side]
    for d in range(1, SIDE):
        peer, device = at_side(d)
        copy(
            local_gram.at[peer], gram_1.at[peer], sem_g1s.at[d], sem_g1r.at[peer], device
        ).wait_recv()
        total = total + gram_1[peer]
    gram_2[at_y] = total
    for n, d in enumerate((-3, -2, -1)):
        gram_copy_2(n, d).start()

    for c in range(CHUNKS):
        pass_on(c)
        share(c)
    prepare(2, window[2])
    for n, d in enumerate((3, 2, 1)):
        at, device = along_y(d)
        copy(
            gram_2.at[at], gram_2.at[at], sem_g2s.at[n], sem_g2r.at[at], device
        ).wait_recv()
    gram_3[side] = gram_2[0] + gram_2[1] + gram_2[2] + gram_2[3]
    for d in range(1, SIDE):
        gram_copy_3(d).start()

    for slot in (1, 3):
        for c in range(CHUNKS):
            copy(
                window.at[2, chunk(c)], window.at[slot, chunk(c)],
                sem_ws.at[0, c], sem_wr.at[slot - 1, c], (other_core, split),
            ).wait_recv()
        prepare(slot, window[slot])
    for d in range(1, SIDE):
        peer, device = at_side(d)
        copy(
            gram_3.at[peer], gram_3.at[peer], sem_g3s.at[d], sem_g3r.at[peer], device
        ).wait_recv()
    eye = lax.broadcasted_iota(jnp.int32, (EMB, EMB), 0)
    eye = eye == lax.broadcasted_iota(jnp.int32, (EMB, EMB), 1)
    base = gram_3[...].reshape(EMB, EMB) + jnp.where(eye, RIDGE, 0.0)

    send_pair.wait_recv()
    both = pair_a[pl.ds(0, SENT)] + recv_b[pl.ds(0, SENT)]
    weights = both[: 2 * SLOTS].reshape(2, SLOTS, EMB)
    block_row = jnp.broadcast_to(both[2 * SLOTS : 2 * SLOTS + 1], (SLOTS, EMB))
    rows_16 = lax.broadcasted_iota(jnp.int32, (SLOTS, EMB), 0)
    lanes_16 = lax.broadcasted_iota(jnp.int32, (SLOTS, EMB), 1)
    block_col = jnp.sum(jnp.where(rows_16 == lanes_16, block_row, 0.0), axis=1, keepdims=True)

    def weighted(slot):
        base_row = 4 * slot
        parts = []
        for u in range(2):
            wishes = weights[u] + block_col
            parts.append(
                jnp.concatenate(
                    [
                        window_t[slot, :, pl.ds(b * EMB, EMB)]
                        * weights[u, base_row + b : base_row + b + 1]
                        for b in range(4)
                    ],
                    axis=1,
                )
            )
            wish = jnp.concatenate(
                [wishes[base_row + b : base_row + b + 1] for b in range(4)], axis=1
            )
            parts.append(jnp.broadcast_to(wish, (8, ROWS)))
        return three_products(jnp.concatenate(parts, axis=0), slot)

    system = weighted(0)
    for slot in range(1, STEPS):
        system = system + weighted(slot)

    def over(value):
        return jnp.sum(value, axis=1, keepdims=True)

    stride = EMB + 8
    matrices = [system[u * stride : u * stride + EMB] + base for u in range(2)]
    right = jnp.concatenate(
        [system[u * stride + EMB : (u + 1) * stride] for u in range(2)], axis=0
    )
    answer = jnp.zeros_like(right)
    residual = right
    direction = right
    norm_now = over(residual * residual)
    for _ in range(CG_ITERS):
        image = jnp.concatenate(
            [
                jnp.dot(
                    direction[8 * u : 8 * u + 8], matrices[u],
                    precision=lax.Precision.HIGHEST, preferred_element_type=F32,
                )
                for u in range(2)
            ],
            axis=0,
        )
        step_size = norm_now / over(direction * image)
        answer = answer + step_size * direction
        residual = residual - step_size * image
        norm_next = over(residual * residual)
        direction = residual + (norm_next / norm_now) * direction
        norm_now = norm_next
    result[2 * at_z] = answer[:1]
    result[2 * at_z + 1] = answer[8:9]

    def answer_copy(d):
        return copy(
            result.at[pl.ds(2 * at_z, 2)], result.at[pl.ds(2 * at_z, 2)],
            sem_xs.at[d], sem_xr.at[at_z], (item, y_hi * Z + at_depth(d)),
        )

    for d in FAR_FIRST:
        answer_copy(d).start()

    for c in range(CHUNKS):
        own_next(c).wait_send()
        relay_core(c, 1, 1).wait_send()
        relay_next(c).wait_send()
    for d in range(1, Z):
        depth_copy(d).wait_send()
    send_pair.wait_send()
    for d in range(1, SIDE):
        gram_copy_1(d).wait_send()
        gram_copy_3(d).wait_send()
    for n, d in enumerate((-3, -2, -1)):
        gram_copy_2(n, d).wait_send()
    for d in range(1, Z):
        peer = at_depth(d)
        copy(
            result.at[pl.ds(2 * peer, 2)], result.at[pl.ds(2 * peer, 2)],
            sem_xs.at[d], sem_xr.at[peer], (item, y_hi * Z + peer),
        ).wait_recv()
    for d in range(1, Z):
        answer_copy(d).wait_send()
    for u in range(USERS):
        out_ref[u : u + 1, :] = result[u]


def body(item_emb, confidences, user_block, item_block, block_age, block_count):
    dma = pltpu.SemaphoreType.DMA
    hbm = pl.BlockSpec(memory_space=pltpu.HBM)
    def hold(value):
        return pltpu.with_memory_space_constraint(value, pltpu.HBM)

    return pl.pallas_call(
        kernel,
        out_shape=jax.ShapeDtypeStruct((USERS, EMB), F32),
        in_specs=[hbm] * 6,
        out_specs=pl.BlockSpec(memory_space=pltpu.VMEM),
        scratch_shapes=[
            pltpu.VMEM((ROWS, EMB), F32),
            pltpu.VMEM((ROWS, EMB), BF16),
            pltpu.VMEM((STEPS, SLOTS), jnp.int32),
            pltpu.VMEM((STEPS, SLOTS), jnp.int32),
            pltpu.VMEM((STEPS, SLOTS), jnp.int32),
            pltpu.VMEM((1, STEPS), jnp.int32),
            pltpu.VMEM((Z, HELD, EMB), F32),
            pltpu.VMEM((Z, HELD, EMB), F32),
            pltpu.VMEM((HELD, EMB), F32),
            pltpu.VMEM((HELD, EMB), F32),
            pltpu.VMEM((STEPS, ROWS, EMB), F32),
            pltpu.VMEM((STEPS, EMB, ROWS), F32),
            pltpu.VMEM((STEPS, ROWS, 2 * EMB), BF16),
            pltpu.VMEM((SIDE, BLOCK, EMB), F32),
            pltpu.VMEM((SIDE, BLOCK, EMB), F32),
            pltpu.VMEM((Y, BLOCK, EMB), F32),
            pltpu.VMEM((SIDE, BLOCK, EMB), F32),
            pltpu.VMEM((USERS, 1, EMB), F32),
            dma((6,)), dma((Z,)), dma((Z,)), dma(()), dma(()),
            dma((3, CHUNKS)), dma((3, CHUNKS)),
            dma((SIDE,)), dma((SIDE,)), dma((Y,)), dma((Y,)), dma((SIDE,)), dma((SIDE,)),
            dma((Z,)), dma((Z,)),
        ],
        compiler_params=pltpu.CompilerParams(
            collective_id=0, has_side_effects=True, vmem_limit_bytes=32 << 20
        ),
        name="als_half_sweep",
    )(
        hold(item_emb),
        hold(confidences.reshape(ROWS, EMB)),
        hold(user_block.reshape(STEPS, SLOTS)),
        hold(item_block.reshape(STEPS, SLOTS)),
        hold(block_age.reshape(STEPS, SLOTS)),
        hold(block_count.reshape(1, STEPS)),
    )


def solution(mesh):
    placed = (
        P("item", None),
        P("item", "split", None, None, None, None),
        P("item", "split", None, None),
        P("item", "split", None, None),
        P("item", "split", None, None),
        P("item", "split", None),
    )
    return jax.shard_map(
        body, mesh=mesh, in_specs=placed, out_specs=P("item", None), check_vma=False
    )
```

time: 51.3 us -> 45.3 us (0.88)
  Pallas kernels: 47.9 us -> 44 us
  local copies, waits for them, and re-layouts: 3.16 us -> 0.6 us
    pallas_call x1, Pallas kernels: 47.9 us -> 44 us  [body(): pl.pallas_call(kernel, out_shape=jax.ShapeDtypeStruct((USERS, EMB), F32),...]
    unnamed x13 -> x1, local copies, waits for them, and re-layouts: 3.16 us -> 0.6 us
where the time goes in v2:
time: 45.3 us; the launch traced here: 44.7 us
  Pallas kernels  44 us (97%)
  local copies, waits for them, and re-layouts  0.6 us (1%)
    pallas_call x1, Pallas kernels, body(): pl.pallas_call(kernel, out_shape=jax.ShapeDtypeStruct((USERS, EMB), F32),...  44 us

profile of v2, /device:TPU:1, one launch (start us, length us, event | category | flops | bytes accessed | tf_op | source)
XLA Modules:
  0.0 44.7 jit_solution(10763416923917820865)
XLA Ops:
  0.0 44.0 %als_half_sweep.1 = f32[24,128]{1,0:T(8,128)S(1)} custom-call(f32[512,128]{1,0:T(8,128)} %emb_hbm.1, bf16[512,128]{1,0:T(8,128)(2,1)} %bitcast.5, s32[4,16]{1,0:T(4,128)} %bitcast.6, s32[4,16]{1,0:T(4,128)} %bitcast.7, s32[4,16]{1,0:T(4,128)} %bitcast.8, s32[1,4]{1,0:T(1,128)} %bitcast.9), custom_call_target="tpu_custom_call" | custom-call | tf_op jit(solution)/shard_map/als_half_sweep/pallas_call | solution.py:432
  44.1 0.6 %copy.8 = f32[24,128]{1,0:T(8,128)} copy(f32[24,128]{1,0:T(8,128)S(1)} %als_half_sweep.1) | data formatting | bytes 24576

commit v3 on v2

--- a/solution.py
+++ b/solution.py
@@ -14,8 +14,9 @@
 X, Y, C = 4, 4, 2
 N_ITEM = X * Y * C
 Z = 12
-SIDE = X * C
-BLOCK = EMB // SIDE
+NEAR = Y * C
+BLOCK = EMB // NEAR
+NEARBY = ((3, 0), (3, 1), (2, 0), (2, 1), (1, 0), (1, 1), (0, 1))
 CHUNKS = 2
 CHUNK = ROWS // CHUNKS
 RIDGE = 0.1
@@ -60,9 +61,9 @@
     item = lax.axis_index("item")
     split = lax.axis_index("split")
     core = lax.rem(item, C)
-    at_x = item // (Y * C)
-    at_y = lax.rem(item, Y * C) // C
-    side = at_x * C + core
+    near = lax.rem(item, NEAR)
+    at_x = item // NEAR
+    at_y = near // C
     y_hi = split // Z
     at_z = lax.rem(split, Z)
     partner = (1 - y_hi) * Z + at_z
@@ -79,14 +80,14 @@
     def at_depth(d):
         return lax.rem(at_z + d, Z)
 
-    def at_side(d):
-        peer = lax.rem(side + d, SIDE)
-        return peer, (peer // C * (Y * C) + at_y * C + lax.rem(peer, C), split)
-
-    def along_y(d):
-        place = lax.rem(y_hi * Y + at_y + d + 2 * Y, 2 * Y)
-        at = lax.rem(place, Y)
-        return at, (at_x * (Y * C) + at * C + core, place // Y * Z + at_z)
+    def along_y(step, turn):
+        place = lax.rem(y_hi * Y + at_y + step + 2 * Y, 2 * Y)
+        peer = lax.rem(place, Y) * C + lax.rem(core + turn, C)
+        return peer, (at_x * NEAR + peer, place // Y * Z + at_z)
+
+    def along_x(d):
+        peer = lax.rem(at_x + d, X)
+        return peer, (peer * NEAR + near, split)
 
     barrier = pltpu.get_barrier_semaphore()
 
@@ -96,10 +97,12 @@
     for d in FAR_FIRST:
         greet((item, y_hi * Z + at_depth(d)))
     greet((item, partner))
-    for d in (1, 2, 3, -1, -2, -3):
-        greet(along_y(d)[1])
-    for d in range(1, SIDE):
-        greet(at_side(d)[1])
+    for step, turn in NEARBY:
+        greet(along_y(-step, turn)[1])
+        if step:
+            greet(along_y(step, turn)[1])
+    for d in range(1, X):
+        greet(along_x(d)[1])
     greet((next_item, next_split))
     greet((prev_item, prev_split))
 
@@ -189,9 +192,9 @@
 
     loads[5].wait()
     turned = prepare(0, emb_ref[...])
-    local_gram[...] = three_products(turned, 0).reshape(SIDE, BLOCK, EMB)
-
-    pl.semaphore_wait(barrier, Z - 1 + 1 + 6 + SIDE - 1 + 3)
+    local_gram[...] = three_products(turned, 0).reshape(NEAR, BLOCK, EMB)
+
+    pl.semaphore_wait(barrier, Z - 1 + 1 + 13 + X - 1 + 3)
 
     def chunk(c):
         return pl.ds(c * CHUNK, CHUNK)
@@ -243,26 +246,27 @@
             sem_as.at[d], sem_ar.at[at_z], (item, y_hi * Z + peer),
         )
 
-    def gram_copy_1(d):
-        peer, device = at_side(d)
-        return copy(
-            local_gram.at[peer], gram_1.at[side], sem_g1s.at[d], sem_g1r.at[side], device
-        )
-
-    def gram_copy_2(n, d):
-        return copy(
-            gram_2.at[at_y], gram_2.at[at_y], sem_g2s.at[n], sem_g2r.at[at_y], along_y(d)[1]
-        )
-
-    def gram_copy_3(d):
-        return copy(
-            gram_3.at[side], gram_3.at[side], sem_g3s.at[d], sem_g3r.at[side], at_side(d)[1]
+    def gram_copy_1(n):
+        peer, device = along_y(-NEARBY[n][0], NEARBY[n][1])
+        return copy(
+            local_gram.at[peer], gram_1.at[near], sem_g1s.at[n], sem_g1r.at[near], device
+        )
+
+    def gram_copy_2(d):
+        return copy(
+            gram_2.at[at_x], gram_2.at[at_x], sem_g2s.at[d], sem_g2r.at[at_x], along_x(d)[1]
+        )
+
+    def gram_copy_3(n):
+        device = along_y(-NEARBY[n][0], NEARBY[n][1])[1]
+        return copy(
+            gram_3.at[near], gram_3.at[near], sem_g3s.at[n], sem_g3r.at[near], device
         )
 
     for d in FAR_FIRST:
         depth_copy(d).start()
-    for d in range(1, SIDE):
-        gram_copy_1(d).start()
+    for n in range(NEAR - 1):
+        gram_copy_1(n).start()
     for c in range(CHUNKS):
         own_next(c).start()
 
@@ -270,6 +274,22 @@
     def _():
         for c in range(CHUNKS):
             own_core(c).start()
+
+    total = local_gram[near]
+    for n, (step, turn) in enumerate(NEARBY):
+        peer, device = along_y(step, turn)
+        copy(
+            local_gram.at[peer], gram_1.at[peer], sem_g1s.at[n], sem_g1r.at[peer], device
+        ).wait_recv()
+        total = total + gram_1[peer]
+    gram_2[at_x] = total
+    for d in range(1, X):
+        gram_copy_2(d).start()
+
+    pass_on(0)
+
+    for c in range(1, CHUNKS):
+        pass_on(c)
 
     def sum_z(d, total):
         peer = at_depth(d)
@@ -285,30 +305,19 @@
     )
     send_pair.start()
 
-    total = local_gram[side]
-    for d in range(1, SIDE):
-        peer, device = at_side(d)
+    for c in range(CHUNKS):
+        share(c)
+
+    for d in range(1, X):
+        peer, device = along_x(d)
         copy(
-            local_gram.at[peer], gram_1.at[peer], sem_g1s.at[d], sem_g1r.at[peer], device
+            gram_2.at[peer], gram_2.at[peer], sem_g2s.at[d], sem_g2r.at[peer], device
         ).wait_recv()
-        total = total + gram_1[peer]
-    gram_2[at_y] = total
-    for n, d in enumerate((-3, -2, -1)):
-        gram_copy_2(n, d).start()
-
-    for c in range(CHUNKS):
-        pass_on(c)
-        share(c)
+    gram_3[near] = gram_2[0] + gram_2[1] + gram_2[2] + gram_2[3]
+    for n in range(NEAR - 1):
+        gram_copy_3(n).start()
+
     prepare(2, window[2])
-    for n, d in enumerate((3, 2, 1)):
-        at, device = along_y(d)
-        copy(
-            gram_2.at[at], gram_2.at[at], sem_g2s.at[n], sem_g2r.at[at], device
-        ).wait_recv()
-    gram_3[side] = gram_2[0] + gram_2[1] + gram_2[2] + gram_2[3]
-    for d in range(1, SIDE):
-        gram_copy_3(d).start()
-
     for slot in (1, 3):
         for c in range(CHUNKS):
             copy(
@@ -316,10 +325,10 @@
                 sem_ws.at[0, c], sem_wr.at[slot - 1, c], (other_core, split),
             ).wait_recv()
         prepare(slot, window[slot])
-    for d in range(1, SIDE):
-        peer, device = at_side(d)
+    for n, (step, turn) in enumerate(NEARBY):
+        peer, device = along_y(step, turn)
         copy(
-            gram_3.at[peer], gram_3.at[peer], sem_g3s.at[d], sem_g3r.at[peer], device
+            gram_3.at[peer], gram_3.at[peer], sem_g3s.at[n], sem_g3r.at[peer], device
         ).wait_recv()
     eye = lax.broadcasted_iota(jnp.int32, (EMB, EMB), 0)
     eye = eye == lax.broadcasted_iota(jnp.int32, (EMB, EMB), 1)
@@ -406,11 +415,11 @@
     for d in range(1, Z):
         depth_copy(d).wait_send()
     send_pair.wait_send()
-    for d in range(1, SIDE):
-        gram_copy_1(d).wait_send()
-        gram_copy_3(d).wait_send()
-    for n, d in enumerate((-3, -2, -1)):
-        gram_copy_2(n, d).wait_send()
+    for n in range(NEAR - 1):
+        gram_copy_1(n).wait_send()
+        gram_copy_3(n).wait_send()
+    for d in range(1, X):
+        gram_copy_2(d).wait_send()
     for d in range(1, Z):
         peer = at_depth(d)
         copy(
@@ -448,14 +457,14 @@
             pltpu.VMEM((STEPS, ROWS, EMB), F32),
             pltpu.VMEM((STEPS, EMB, ROWS), F32),
             pltpu.VMEM((STEPS, ROWS, 2 * EMB), BF16),
-            pltpu.VMEM((SIDE, BLOCK, EMB), F32),
-            pltpu.VMEM((SIDE, BLOCK, EMB), F32),
-            pltpu.VMEM((Y, BLOCK, EMB), F32),
-            pltpu.VMEM((SIDE, BLOCK, EMB), F32),
+            pltpu.VMEM((NEAR, BLOCK, EMB), F32),
+            pltpu.VMEM((NEAR, BLOCK, EMB), F32),
+            pltpu.VMEM((X, BLOCK, EMB), F32),
+            pltpu.VMEM((NEAR, BLOCK, EMB), F32),
             pltpu.VMEM((USERS, 1, EMB), F32),
             dma((6,)), dma((Z,)), dma((Z,)), dma(()), dma(()),
             dma((3, CHUNKS)), dma((3, CHUNKS)),
-            dma((SIDE,)), dma((SIDE,)), dma((Y,)), dma((Y,)), dma((SIDE,)), dma((SIDE,)),
+            dma((NEAR,)), dma((NEAR,)), dma((X,)), dma((X,)), dma((NEAR,)), dma((NEAR,)),
             dma((Z,)), dma((Z,)),
         ],
         compiler_params=pltpu.CompilerParams(

time: 45.3 us -> 43.5 us (0.960)
  the two profiles are of different devices: /device:TPU:1 before, /device:TPU:8 now
where the time goes in v3:
time: 43.5 us; the launch traced here: 43.3 us
  Pallas kernels  42.7 us (98%)
  local copies, waits for them, and re-layouts  0.6 us (1%)
    pallas_call x1, Pallas kernels, body(): pl.pallas_call(kernel, out_shape=jax.ShapeDtypeStruct((USERS, EMB), F32),...  42.7 us

profile of v3, /device:TPU:8, one launch (start us, length us, event | category | flops | bytes accessed | tf_op | source)
XLA Modules:
  0.0 43.3 jit_solution(9126513988501663837)
XLA Ops:
  0.0 42.7 %als_half_sweep.1 = f32[24,128]{1,0:T(8,128)S(1)} custom-call(f32[512,128]{1,0:T(8,128)} %emb_hbm.1, bf16[512,128]{1,0:T(8,128)(2,1)} %bitcast.5, s32[4,16]{1,0:T(4,128)} %bitcast.6, s32[4,16]{1,0:T(4,128)} %bitcast.7, s32[4,16]{1,0:T(4,128)} %bitcast.8, s32[1,4]{1,0:T(1,128)} %bitcast.9), custom_call_target="tpu_custom_call" | custom-call | tf_op jit(solution)/shard_map/als_half_sweep/pallas_call | solution.py:441
  42.7 0.6 %copy.8 = f32[24,128]{1,0:T(8,128)} copy(f32[24,128]{1,0:T(8,128)S(1)} %als_half_sweep.1) | data formatting | bytes 24576

commit v4 on v3

--- a/solution.py
+++ b/solution.py
@@ -15,7 +15,8 @@
 N_ITEM = X * Y * C
 Z = 12
 NEAR = Y * C
-BLOCK = EMB // NEAR
+OWNERS = 2 * C
+BLOCK = EMB // OWNERS
 NEARBY = ((3, 0), (3, 1), (2, 0), (2, 1), (1, 0), (1, 1), (0, 1))
 CHUNKS = 2
 CHUNK = ROWS // CHUNKS
@@ -85,6 +86,14 @@
         peer = lax.rem(place, Y) * C + lax.rem(core + turn, C)
         return peer, (at_x * NEAR + peer, place // Y * Z + at_z)
 
+    owner = near - C
+    owns = jnp.logical_and(at_y >= 1, at_y <= 2)
+
+    def owner_at(n, sign):
+        step = lax.rem(sign * (1 + n // C - at_y) + 2 * Y, Y)
+        place = lax.rem(y_hi * Y + at_y + sign * step + 2 * Y, 2 * Y)
+        return at_x * NEAR + (1 + n // C) * C + n % C, place // Y * Z + at_z
+
     def along_x(d):
         peer = lax.rem(at_x + d, X)
         return peer, (peer * NEAR + near, split)
@@ -192,7 +201,7 @@
 
     loads[5].wait()
     turned = prepare(0, emb_ref[...])
-    local_gram[...] = three_products(turned, 0).reshape(NEAR, BLOCK, EMB)
+    local_gram[...] = three_products(turned, 0).reshape(OWNERS, BLOCK, EMB)
 
     pl.semaphore_wait(barrier, Z - 1 + 1 + 13 + X - 1 + 3)
 
@@ -247,9 +256,8 @@
         )
 
     def gram_copy_1(n):
-        peer, device = along_y(-NEARBY[n][0], NEARBY[n][1])
-        return copy(
-            local_gram.at[peer], gram_1.at[near], sem_g1s.at[n], sem_g1r.at[near], device
+        return copy(
+            local_gram.at[n], gram_1.at[near], sem_g1s.at[n], sem_g1r.at[near], owner_at(n, -1)
         )
 
     def gram_copy_2(d):
@@ -260,13 +268,19 @@
     def gram_copy_3(n):
         device = along_y(-NEARBY[n][0], NEARBY[n][1])[1]
         return copy(
-            gram_3.at[near], gram_3.at[near], sem_g3s.at[n], sem_g3r.at[near], device
-        )
+            gram_3.at[owner], gram_3.at[owner], sem_g3s.at[n], sem_g3r.at[owner], device
+        )
+
+    def for_other_owners(act):
+        for n in range(OWNERS):
+
+            @pl.when(owner != n)
+            def _():
+                act(n)
 
     for d in FAR_FIRST:
         depth_copy(d).start()
-    for n in range(NEAR - 1):
-        gram_copy_1(n).start()
+    for_other_owners(lambda n: gram_copy_1(n).start())
     for c in range(CHUNKS):
         own_next(c).start()
 
@@ -275,16 +289,18 @@
         for c in range(CHUNKS):
             own_core(c).start()
 
-    total = local_gram[near]
-    for n, (step, turn) in enumerate(NEARBY):
-        peer, device = along_y(step, turn)
-        copy(
-            local_gram.at[peer], gram_1.at[peer], sem_g1s.at[n], sem_g1r.at[peer], device
-        ).wait_recv()
-        total = total + gram_1[peer]
-    gram_2[at_x] = total
-    for d in range(1, X):
-        gram_copy_2(d).start()
+    @pl.when(owns)
+    def _():
+        total = local_gram[owner]
+        for step, turn in NEARBY:
+            peer, device = along_y(step, turn)
+            copy(
+                local_gram.at[0], gram_1.at[peer], sem_g1s.at[0], sem_g1r.at[peer], device
+            ).wait_recv()
+            total = total + gram_1[peer]
+        gram_2[at_x] = total
+        for d in range(1, X):
+            gram_copy_2(d).start()
 
     pass_on(0)
 
@@ -308,14 +324,16 @@
     for c in range(CHUNKS):
         share(c)
 
-    for d in range(1, X):
-        peer, device = along_x(d)
-        copy(
-            gram_2.at[peer], gram_2.at[peer], sem_g2s.at[d], sem_g2r.at[peer], device
-        ).wait_recv()
-    gram_3[near] = gram_2[0] + gram_2[1] + gram_2[2] + gram_2[3]
-    for n in range(NEAR - 1):
-        gram_copy_3(n).start()
+    @pl.when(owns)
+    def _():
+        for d in range(1, X):
+            peer, device = along_x(d)
+            copy(
+                gram_2.at[peer], gram_2.at[peer], sem_g2s.at[d], sem_g2r.at[peer], device
+            ).wait_recv()
+        gram_3[owner] = gram_2[0] + gram_2[1] + gram_2[2] + gram_2[3]
+        for n in range(NEAR - 1):
+            gram_copy_3(n).start()
 
     prepare(2, window[2])
     for slot in (1, 3):
@@ -325,11 +343,11 @@
                 sem_ws.at[0, c], sem_wr.at[slot - 1, c], (other_core, split),
             ).wait_recv()
         prepare(slot, window[slot])
-    for n, (step, turn) in enumerate(NEARBY):
-        peer, device = along_y(step, turn)
-        copy(
-            gram_3.at[peer], gram_3.at[peer], sem_g3s.at[n], sem_g3r.at[peer], device
+    for_other_owners(
+        lambda n: copy(
+            gram_3.at[n], gram_3.at[n], sem_g3s.at[0], sem_g3r.at[n], owner_at(n, 1)
         ).wait_recv()
+    )
     eye = lax.broadcasted_iota(jnp.int32, (EMB, EMB), 0)
     eye = eye == lax.broadcasted_iota(jnp.int32, (EMB, EMB), 1)
     base = gram_3[...].reshape(EMB, EMB) + jnp.where(eye, RIDGE, 0.0)
@@ -415,11 +433,15 @@
     for d in range(1, Z):
         depth_copy(d).wait_send()
     send_pair.wait_send()
-    for n in range(NEAR - 1):
-        gram_copy_1(n).wait_send()
-        gram_copy_3(n).wait_send()
-    for d in range(1, X):
-        gram_copy_2(d).wait_send()
+    for_other_owners(lambda n: gram_copy_1(n).wait_send())
+
+    @pl.when(owns)
+    def _():
+        for n in range(NEAR - 1):
+            gram_copy_3(n).wait_send()
+        for d in range(1, X):
+            gram_copy_2(d).wait_send()
+
     for d in range(1, Z):
         peer = at_depth(d)
         copy(
@@ -457,14 +479,14 @@
             pltpu.VMEM((STEPS, ROWS, EMB), F32),
             pltpu.VMEM((STEPS, EMB, ROWS), F32),
             pltpu.VMEM((STEPS, ROWS, 2 * EMB), BF16),
-            pltpu.VMEM((NEAR, BLOCK, EMB), F32),
+            pltpu.VMEM((OWNERS, BLOCK, EMB), F32),
             pltpu.VMEM((NEAR, BLOCK, EMB), F32),
             pltpu.VMEM((X, BLOCK, EMB), F32),
-            pltpu.VMEM((NEAR, BLOCK, EMB), F32),
+            pltpu.VMEM((OWNERS, BLOCK, EMB), F32),
             pltpu.VMEM((USERS, 1, EMB), F32),
             dma((6,)), dma((Z,)), dma((Z,)), dma(()), dma(()),
             dma((3, CHUNKS)), dma((3, CHUNKS)),
-            dma((NEAR,)), dma((NEAR,)), dma((X,)), dma((X,)), dma((NEAR,)), dma((NEAR,)),
+            dma((OWNERS,)), dma((NEAR,)), dma((X,)), dma((X,)), dma((NEAR,)), dma((OWNERS,)),
             dma((Z,)), dma((Z,)),
         ],
         compiler_params=pltpu.CompilerParams(

time: 43.5 us -> 42.6 us (0.979)
  the two profiles are of different devices: /device:TPU:8 before, /device:TPU:1 now
where the time goes in v4:
time: 42.6 us; the launch traced here: 42.4 us
  Pallas kernels  41.8 us (98%)
  local copies, waits for them, and re-layouts  0.6 us (1%)
    pallas_call x1, Pallas kernels, body(): pl.pallas_call(kernel, out_shape=jax.ShapeDtypeStruct((USERS, EMB), F32),...  41.8 us

profile of v4, /device:TPU:1, one launch (start us, length us, event | category | flops | bytes accessed | tf_op | source)
XLA Modules:
  0.0 42.4 jit_solution(12992047208335372270)
XLA Ops:
  0.0 41.8 %als_half_sweep.1 = f32[24,128]{1,0:T(8,128)S(1)} custom-call(f32[512,128]{1,0:T(8,128)} %emb_hbm.1, bf16[512,128]{1,0:T(8,128)(2,1)} %bitcast.5, s32[4,16]{1,0:T(4,128)} %bitcast.6, s32[4,16]{1,0:T(4,128)} %bitcast.7, s32[4,16]{1,0:T(4,128)} %bitcast.8, s32[1,4]{1,0:T(1,128)} %bitcast.9), custom_call_target="tpu_custom_call" | custom-call | tf_op jit(solution)/shard_map/als_half_sweep/pallas_call | solution.py:463
  41.8 0.6 %copy.8 = f32[24,128]{1,0:T(8,128)} copy(f32[24,128]{1,0:T(8,128)S(1)} %als_half_sweep.1) | data formatting | bytes 24576

commit v5 on v4

--- a/solution.py
+++ b/solution.py
@@ -307,15 +307,15 @@
     for c in range(1, CHUNKS):
         pass_on(c)
 
-    def sum_z(d, total):
+    total = send_a[at_z, pl.ds(0, SENT)]
+    for d in reversed(FAR_FIRST):
         peer = at_depth(d)
         copy(
             send_a.at[0, pl.ds(0, SENT)], recv_a.at[peer, pl.ds(0, SENT)],
             sem_as.at[d], sem_ar.at[peer], (item, y_hi * Z + peer),
         ).wait_recv()
-        return total + recv_a[peer, pl.ds(0, SENT)]
-
-    pair_a[pl.ds(0, SENT)] = lax.fori_loop(1, Z, sum_z, send_a[at_z, pl.ds(0, SENT)])
+        total = total + recv_a[peer, pl.ds(0, SENT)]
+    pair_a[pl.ds(0, SENT)] = total
     send_pair = copy(
         pair_a.at[pl.ds(0, SENT)], recv_b.at[pl.ds(0, SENT)], sem_bs, sem_br, (item, partner)
     )
@@ -397,17 +397,16 @@
     residual = right
     direction = right
     norm_now = over(residual * residual)
+    pieces = [jnp.concatenate(high_low(matrix), axis=1) for matrix in matrices]
     for _ in range(CG_ITERS):
-        image = jnp.concatenate(
-            [
-                jnp.dot(
-                    direction[8 * u : 8 * u + 8], matrices[u],
-                    precision=lax.Precision.HIGHEST, preferred_element_type=F32,
-                )
-                for u in range(2)
-            ],
-            axis=0,
-        )
+        left = jnp.concatenate(high_low(direction), axis=0)
+        image = []
+        for u in range(2):
+            out = jnp.dot(left, pieces[u], preferred_element_type=F32)
+            rows = slice(8 * u, 8 * u + 8)
+            rest = slice(16 + 8 * u, 24 + 8 * u)
+            image.append(out[rows, :EMB] + out[rows, EMB:] + out[rest, :EMB])
+        image = jnp.concatenate(image, axis=0)
         step_size = norm_now / over(direction * image)
         answer = answer + step_size * direction
         residual = residual - step_size * image

time: 42.6 us -> 42.2 us (level)
  no operation moved by 1% of the time
where the time goes in v5:
time: 42.2 us; the launch traced here: 42.1 us
  Pallas kernels  41.5 us (98%)
  local copies, waits for them, and re-layouts  0.6 us (1%)
    pallas_call x1, Pallas kernels, body(): pl.pallas_call(kernel, out_shape=jax.ShapeDtypeStruct((USERS, EMB), F32),...  41.5 us

profile of v5, /device:TPU:1, one launch (start us, length us, event | category | flops | bytes accessed | tf_op | source)
XLA Modules:
  0.0 42.1 jit_solution(10559690066152274228)
XLA Ops:
  0.0 41.5 %als_half_sweep.1 = f32[24,128]{1,0:T(8,128)S(1)} custom-call(f32[512,128]{1,0:T(8,128)} %emb_hbm.1, bf16[512,128]{1,0:T(8,128)(2,1)} %bitcast.5, s32[4,16]{1,0:T(4,128)} %bitcast.6, s32[4,16]{1,0:T(4,128)} %bitcast.7, s32[4,16]{1,0:T(4,128)} %bitcast.8, s32[1,4]{1,0:T(1,128)} %bitcast.9), custom_call_target="tpu_custom_call" | custom-call | tf_op jit(solution)/shard_map/als_half_sweep/pallas_call | solution.py:462
  41.5 0.6 %copy.8 = f32[24,128]{1,0:T(8,128)} copy(f32[24,128]{1,0:T(8,128)S(1)} %als_half_sweep.1) | data formatting | bytes 24576

commit v6 on v5

--- a/solution.py
+++ b/solution.py
@@ -233,15 +233,15 @@
         )
 
     def pass_on(c):
-        own_next(c).wait_recv()
-
         @pl.when(core == 1)
         def _():
+            own_next(c).wait_recv()
             relay_next(c).start()
 
     def share(c):
         @pl.when(core == 0)
         def _():
+            own_next(c).wait_recv()
             relay_core(c, 3, 2).start()
 
         @pl.when(core == 1)

time: 42.2 us -> 42.1 us (level)
  no operation moved by 1% of the time
where the time goes in v6:
time: 42.1 us; the launch traced here: 42 us
  Pallas kernels  41.4 us (98%)
  local copies, waits for them, and re-layouts  0.6 us (1%)
    pallas_call x1, Pallas kernels, body(): pl.pallas_call(kernel, out_shape=jax.ShapeDtypeStruct((USERS, EMB), F32),...  41.4 us

profile of v6, /device:TPU:1, one launch (start us, length us, event | category | flops | bytes accessed | tf_op | source)
XLA Modules:
  0.0 42.0 jit_solution(3015320675619763914)
XLA Ops:
  0.0 41.4 %als_half_sweep.1 = f32[24,128]{1,0:T(8,128)S(1)} custom-call(f32[512,128]{1,0:T(8,128)} %emb_hbm.1, bf16[512,128]{1,0:T(8,128)(2,1)} %bitcast.5, s32[4,16]{1,0:T(4,128)} %bitcast.6, s32[4,16]{1,0:T(4,128)} %bitcast.7, s32[4,16]{1,0:T(4,128)} %bitcast.8, s32[1,4]{1,0:T(1,128)} %bitcast.9), custom_call_target="tpu_custom_call" | custom-call | tf_op jit(solution)/shard_map/als_half_sweep/pallas_call | solution.py:462
  41.4 0.6 %copy.8 = f32[24,128]{1,0:T(8,128)} copy(f32[24,128]{1,0:T(8,128)S(1)} %als_half_sweep.1) | data formatting | bytes 24576
